TPU v7x, 32 devices: a whole 2x2x4 slice. The times are simulated.
32 devices in a mesh: groups: 2 (over x), rows: 8 (over z, y), cols: 2 (over core).
Axes of the slice: x: 2, y: 2, z: 4, core: 2. Of those that a mesh axis runs over, the one named last changes fastest.
Arguments:
- radiosity: bfloat16 [4, 98304], P(None, ('groups', 'rows', 'cols')), parts along dimension 1, may hold values from 0.099609375 to 4
- emission: float32 [4, 98304], P(None, ('groups', 'rows', 'cols')), parts along dimension 1, may hold values from 0.05 to 2
- material: int32 [98304], P(('groups', 'rows', 'cols')), parts along dimension 0, may hold values from 0 to 15
- reflectance: float32 [4, 16], replicated, may hold values from 0.1 to 0.9
- static_tiles: bfloat16 [16, 2, 64, 128, 128], P(('groups', 'rows'), 'cols'), parts along dimension 0, may hold values from 0.00019931793 to 0.0079956055
- static_index: int32 [16, 2, 2, 64], P(('groups', 'rows'), 'cols'), parts along dimension 0, may hold values from 0 to 191, as said below
- row_geometry: float32 [6, 4, 98304], P(None, None, ('groups', 'rows')), parts along dimension 2, as said below
- array_geometry: float32 [4, 8, 6, 4, 4096], P(('groups', 'cols'), 'rows'), parts along dimension 0, as said below
- array_owner: int32 [4], P(('groups', 'cols')), parts along dimension 0, may hold values from 0 to 7
- array_index: int32 [16, 2, 2, 16], P(('groups', 'rows')), parts along dimension 0, may hold values from 0 to 47, as said below
- array_count: int32 [16, 2], P(('groups', 'rows')), parts along dimension 0, may hold values from 1 to 16, as said below
- visibility: int32 [16, 2, 16, 128, 128], P(('groups', 'rows'), 'cols'), parts along dimension 0, may hold values 0 or 1
Outputs:
- new_radiosity: float32 [4, 98304], P(None, ('groups', 'rows', 'cols')), parts along dimension 1
There are 2 independent parts, one for each index of `groups`. A program takes and returns all parts, laid end to end along the dimension named above; an argument that names none is the same for every part. Nothing has to cross between parts.
Inputs may be any that keep to these rules, and one draw needn't show every extreme that they name: `static_index`: within one entry [r, g] the 64 pairs (row tile, column tile) are distinct, row tiles below 48. `array_index`: within one entry [r, g] the 16 pairs (row tile, array tile) are distinct, row tiles below 48, array tiles below 32; slots at or after the count are not used. `array_count`: some entry equals 16 in every draw. `row_geometry`: positions in a box of side 2, areas between 0.005 and 0.05. `array_geometry`: positions in a box of side 2, areas between 0.005 and 0.05.
All inputs are finite; a program needn't handle non-finite values. No bound on the sum of `visibility` on one device may be relied on, other than what follows from the above.
Results may differ from a plain program's by a relative error of at most 0.0003.
Values may be sent and summed in bfloat16 or wider, within the bound.
No kernel may reach another device: no remote copies, remote signals or barrier semaphores. Data moves between devices by JAX's collectives and lax.ppermute only.
A program may use at most 64 MiB of HBM per device.

v0:
```python
import math

import jax
import jax.numpy as jnp
from jax import lax
from jax.sharding import PartitionSpec as P

POINTS = 4


def from_root(value, axis, source):
    kept = jnp.where(lax.axis_index(axis) == source, value, 0).astype(value.dtype)
    return lax.psum(kept, axis)


def unit_normal(polar_angle, azimuth):
    return jnp.stack(
        [
            jnp.sin(polar_angle) * jnp.cos(azimuth),
            jnp.sin(polar_angle) * jnp.sin(azimuth),
            jnp.cos(polar_angle),
        ]
    )


def kernel_tile(row_points, col_points):
    offset = col_points[0:3][:, None, None, :, :] - row_points[0:3][:, :, :, None, None]
    row_normal = unit_normal(row_points[3], row_points[4])
    col_normal = unit_normal(col_points[3], col_points[4])
    facing = jnp.sum(row_normal[:, :, :, None, None] * offset, axis=0)
    toward = jnp.sum(col_normal[:, None, None, :, :] * offset, axis=0)
    spread = jnp.sum(offset * offset, axis=0)
    col_area = col_points[5][None, None, :, :]
    kernel_value = (
        jnp.maximum(facing, 0.0)
        * jnp.maximum(-toward, 0.0)
        * col_area
        / (math.pi * (spread + col_area) ** 2)
    )
    return jnp.sum(kernel_value, axis=(0, 2)) / POINTS


def tile_rows(products, row_ids, row_tiles):
    onehot = (row_ids[:, None] == jnp.arange(row_tiles, dtype=jnp.int32)[None, :]).astype(
        jnp.float32
    )
    return jnp.einsum("kbp,kr->brp", products, onehot, precision=lax.Precision.HIGHEST)


def body(
    radiosity,
    emission,
    material,
    reflectance,
    static_tiles,
    static_index,
    row_geometry,
    array_geometry,
    array_owner,
    array_index,
    array_count,
    visibility,
):
    band_count = radiosity.shape[0]
    tile_size = visibility.shape[-1]
    row_length = row_geometry.shape[2]
    row_tiles = row_length // tile_size
    slot_total = visibility.shape[2]
    own_group = lax.axis_index("cols")
    gathered = lax.all_gather(radiosity, "rows", axis=1, tiled=True)
    column_tiles = gathered.shape[1] // tile_size
    array_tiles = array_geometry.shape[-1] // tile_size
    by_tile = gathered.reshape(band_count, column_tiles, tile_size)
    stored = static_tiles[0, 0]
    positions = static_index[0, 0]
    slices = jnp.take(by_tile, positions[1], axis=1)
    products = jnp.einsum("kps,bks->kbp", stored, slices, preferred_element_type=jnp.float32)
    summed = tile_rows(products, positions[0], row_tiles)
    own_points = from_root(array_geometry[0, 0], "rows", array_owner[0])
    slot_lists = array_index[0]
    live_counts = array_count[0]
    own_list = slot_lists[own_group]
    own_count = live_counts[own_group]
    blank_tiles = jnp.zeros((slot_total, tile_size, tile_size), jnp.float32)

    def row_slab(row_tile):
        return lax.dynamic_slice_in_dim(row_geometry, row_tile * tile_size, tile_size, 2)

    def array_slab(points, array_tile):
        return lax.dynamic_slice_in_dim(points, array_tile * tile_size, tile_size, 2)

    def make_own(slot_index, buffer):
        one_tile = kernel_tile(
            row_slab(own_list[0, slot_index]), array_slab(own_points, own_list[1, slot_index])
        )
        return lax.dynamic_update_index_in_dim(buffer, one_tile, slot_index, 0)

    rebuilt = lax.fori_loop(0, own_count, make_own, blank_tiles)
    live_mask = (jnp.arange(slot_total, dtype=jnp.int32) < own_count).astype(jnp.float32)
    visible = visibility[0, 0].astype(jnp.float32) * live_mask[:, None, None]
    rebuilt = rebuilt * visible
    array_slices = jnp.take(by_tile, column_tiles - array_tiles + own_list[1], axis=1).astype(
        jnp.float32
    )
    array_products = jnp.einsum(
        "kps,bks->kbp", rebuilt, array_slices, precision=lax.Precision.HIGHEST
    )
    summed = summed + tile_rows(array_products, own_list[0], row_tiles)
    shares = lax.psum_scatter(
        summed.reshape(band_count, row_length), "cols", scatter_dimension=1, tiled=True
    )
    material_count = reflectance.shape[1]
    onehot = (jnp.arange(material_count, dtype=jnp.int32)[:, None] == material[None, :]).astype(
        jnp.float32
    )
    albedo = jnp.dot(reflectance, onehot, precision=lax.Precision.HIGHEST)
    return emission + albedo * shares


def solution(mesh):
    in_specs = (
        P(None, ("groups", "rows", "cols")),
        P(None, ("groups", "rows", "cols")),
        P(("groups", "rows", "cols")),
        P(),
        P(("groups", "rows"), "cols", None, None, None),
        P(("groups", "rows"), "cols", None, None),
        P(None, None, ("groups", "rows")),
        P(("groups", "cols"), "rows", None, None, None),
        P(("groups", "cols")),
        P(("groups", "rows"), None, None, None),
        P(("groups", "rows"), None),
        P(("groups", "rows"), "cols", None, None, None),
    )
    out_specs = P(None, ("groups", "rows", "cols"))
    return jax.shard_map(body, mesh=mesh, in_specs=in_specs, out_specs=out_specs, check_vma=False)
```

profile of v0, /device:TPU:0, one launch (start us, length us, event | category | flops | bytes accessed | tf_op | source)
XLA Modules:
  0.0 202.8 jit_solution(8542421547053331783)
XLA Ops:
  7.3 0.9 select_bitcast_fusion
  9.7 0.7 compare_and_fusion.1
  11.0 1.3 constant_dynamic-slice_fusion.9
  13.0 32.8 %all_gather.3 = bf16[4,24576]{1,0:T(4,128)(2,1)S(1)} all-gather(bf16[4,3072]{1,0:T(4,128)(2,1)} %param.14), channel_id=1, replica_groups=mesh['groups'=2,'rows'=8,'cols'=2] {'rows'}, dimensions={1}, use_global_device_ids=true | all-gather | bytes 221184 | tf_op jit(solution)/shard_map/all_gather | solution.py:70
  46.4 1.2 fusion.11
  48.4 36.5 %all-reduce.2.cloned.1.call-done = f32[6,4,4096]{2,1,0:T(4,128)} async-done(((f32[6,4,4096]{2,1,0:T(4,128)}), f32[6,4,4096]{2,1,0:T(4,128)}) %all-reduce.2.cloned.1.call-update) | async-done | bytes 393232 | tf_op jit(solution)/shard_map/psum | solution.py:13
  85.0 23.8 %while.10 = (s32[]{:T(128)}, f32[16,128,128]{2,1,0:T(8,128)S(1)}, s32[]{:T(128)}, s32[2,16]{1,0:T(2,128)S(1)}, f32[6,4,6144]{2,1,0:T(4,128)}, /*index=5*/f32[6,4...) while((s32[]{:T(128)}, f32[16,128,128]{2,1,0:T(8,128)S(1)}, ...), condition=%wide.region_6.7_spmd, body=%wide.region_1.6_spmd.sunk | while | flops 7348240 | bytes 6588771 | solution.py:98
  87.6 0.8 fusion.46
  88.4 0.7 constant_dynamic-slice_fusion.14
  89.1 1.3 fusion.47
  93.4 0.8 fusion.46
  94.2 0.7 constant_dynamic-slice_fusion.14
  94.9 1.3 fusion.47
  99.2 0.8 fusion.46
  100.0 0.7 constant_dynamic-slice_fusion.14
  100.7 1.3 fusion.47
  105.0 0.8 fusion.46
  105.8 0.7 constant_dynamic-slice_fusion.14
  106.5 1.3 fusion.47
  108.8 2.3 %fusion.15 = f32[16,4,128]{2,1,0:T(4,128)S(1)} fusion(f32[16,128,128]{2,1,0:T(8,128)S(1)} %get-tuple-element.38, s32[1,1,16,128,128]{4,3,2,1,0:T(8,128)} %param.25, f32[16]{0:T(128)S(1)} %get-tuple-element.68, bf16[16,4,128]{2,1,0:T(4,128)(2,1)S(1)} %gather_fusion.1, pred[16]{0:T(512)(128)(4,1)S(1)} %get-tuple-element.69), kind=kOutput, calls=%fused_computation.40 | convolution fusion | flops 13377536 | bytes 2146384 | tf_op jit(solution)/shard_map/kps,bks->kbp/dot_general | solution.py:105
  111.4 2.2 %copy.19 = f32[4,48,128]{0,2,1:T(8,128)} copy(f32[4,48,128]{2,1,0:T(8,128)S(1)} %fusion.13) | data formatting | bytes 196608
  113.7 79.6 %reduce-scatter.4.cloned.1.call-done = f32[3072,4]{1,0:T(8,128)} async-done(((f32[6144,4]{1,0:T(8,128)}), f32[3072,4]{1,0:T(8,128)}) %reduce-scatter.4.cloned.1.call-update) | async-done | bytes 49168
  193.2 1.9 copy.18
  195.1 0.8 fusion.10
  (48 shorter events, 8.9 us)
Async XLA Ops:
  6.5 39.9 %copy-start = (bf16[1,1,64,128,128]{4,3,2,1,0:T(8,128)(2,1)S(1)}, bf16[1,1,64,128,128]{4,3,2,1,0:T(8,128)(2,1)}, u32[]{:S(2)}) copy-start(bf16[1,1,64,128,128]{4,3,2,1,0:T(8,128)(2,1)} %param.18) | copy-start | bytes 6291460
  6.5 41.7 %copy-start.4 = (s32[1,2,2,16]{3,2,1,0:T(2,128)S(1)}, s32[1,2,2,16]{3,2,1,0:T(2,128)}, u32[]{:S(2)}) copy-start(s32[1,2,2,16]{3,2,1,0:T(2,128)} %param.23) | copy-start | bytes 772
  6.5 78.4 %all-reduce.2.cloned.1.call-start = ((), (), s32[]{:S(2)}) async-start(), calls=%async_computation.1 | async-start | bytes 786432 | tf_op jit(solution)/shard_map/psum | solution.py:13
  8.2 185.0 %reduce-scatter.4.cloned.1.call-start = ((), (), s32[]{:S(2)}) async-start(), calls=%async_computation.2 | async-start | bytes 4718592
  113.6 81.5 %copy-start.1 = (f32[4,3072]{1,0:T(4,128)S(1)}, f32[4,3072]{1,0:T(4,128)}, u32[]{:S(2)}) copy-start(f32[4,3072]{1,0:T(4,128)} %param.15) | copy-start | bytes 147460
  113.6 81.5 %copy-start.2 = (s32[3072]{0:T(1024)S(1)}, s32[3072]{0:T(1024)}, u32[]{:S(2)}) copy-start(s32[3072]{0:T(1024)} %param.16) | copy-start | bytes 36868
  113.6 81.5 %copy-start.3 = (f32[4,16]{1,0:T(4,128)S(1)}, f32[4,16]{1,0:T(4,128)}, u32[]{:S(2)}) copy-start(f32[4,16]{1,0:T(4,128)} %param.17) | copy-start | bytes 772
Sparse Core Ops, SparseCore 0:
  10.7 74.1 all-reduce.1
  113.8 79.4 reduce-scatter.3
where the time goes:
time: 205 us; the launch traced here: 203 us
  waiting for transfers between devices  116 us (57%)
  blocking collectives  32.8 us (16%)
  between operations  14.3 us (7%)
  local copies, waits for them, and re-layouts  13.6 us (7%)
  other arithmetic  12.8 us (6%)
  loops' own time  8.42 us (4%)
  matrix products  4.8 us (2%)
    unnamed x3, waiting for transfers between devices  79.6 us
    psum x1, waiting for transfers between devices, from_root(): return lax.psum(kept, axis)  36.5 us
    all_gather x1, blocking collectives, body(): gathered = lax.all_gather(radiosity, 'rows', axis=1, tiled=True)  32.8 us
    another operation x1, loops' own time, body(): rebuilt = lax.fori_loop(0, own_count, make_own, blank_tiles)  8.42 us
    reduce_sum x4, other arithmetic, kernel_tile(): facing = jnp.sum(row_normal[:, :, :, None, None] * offset, axis=0)  5.07 us
    unnamed x12, local copies, waits for them, and re-layouts  4.11 us
  transfers between devices with their start and end apart: 2, of which 2 were waited for; matrix products, arithmetic and copies ran while one was open for 4% of the time, Pallas kernels for 0%

commit v1 on v0

v1 whole, which is shorter than its diff:
```python
import functools
import math

import jax
import jax.numpy as jnp
from jax import lax
from jax.experimental import pallas as pl
from jax.experimental.pallas import tpu as pltpu
from jax.sharding import PartitionSpec as P

TILE = 128
POINTS = 4
POS = 2.0**14
MOM = 2.0**19
RAD = 2.0**11
REFS = 8
GROUP = 16 * 12
F32 = jnp.float32
BF16 = jnp.bfloat16
VMEM = pltpu.VMEM
NT = (((1,), (1,)), ((), ()))


def whole(memory_space=VMEM):
    return pl.BlockSpec(memory_space=memory_space)


def parts3(value):
    first = value.astype(BF16)
    rest = value - first.astype(F32)
    second = rest.astype(BF16)
    third = (rest - second.astype(F32)).astype(BF16)
    return first, second, third


def encode_kernel(half_tiles, geo_ref, rad_ref, keep_ref, send_ref, halves):
    lower = lax.axis_index("rows") & 1
    half_rows = 12 * half_tiles + REFS
    angles = jnp.concatenate([geo_ref[3], geo_ref[4]], axis=0)
    sines, cosines = jnp.sin(angles), jnp.cos(angles)
    area = geo_ref[5]
    normal = (
        sines[0:4] * cosines[4:8],
        sines[0:4] * sines[4:8],
        cosines[0:4],
    )
    for axis in range(3):
        place = geo_ref[axis]
        low = jnp.min(jnp.min(place, axis=1, keepdims=True), axis=0, keepdims=True)
        high = jnp.max(jnp.max(place, axis=1, keepdims=True), axis=0, keepdims=True)
        centre = jnp.floor((low + high) * 0.5 + 0.5)
        moved = jnp.floor((place - centre) * POS + 0.5).astype(jnp.int32)
        moved = jnp.clip(moved, -32768, 32767)
        moment = jnp.floor(area * normal[axis] * MOM + 0.5).astype(jnp.int32)
        moment = jnp.clip(moment, -32768, 32767)
        words = (moved << 16) | (moment & 65535)
        for tile in range(2 * half_tiles):
            row = 12 * (tile % half_tiles) + 4 * axis
            halves[tile // half_tiles, row : row + 4, :] = words[:, tile * TILE : (tile + 1) * TILE]
        whole_centre = jnp.broadcast_to(centre.astype(jnp.int32), (1, TILE))
        for half in range(2):
            row = half_rows - REFS + axis
            halves[half, row : row + 1, :] = whole_centre
    for half in range(2):
        halves[half, half_rows - REFS + 3 :, :] = jnp.zeros((REFS - 3, TILE), jnp.int32)
    keep_ref[...] = halves[lower]
    send_ref[0:half_rows, :] = halves[1 - lower]
    rad = (rad_ref[...].astype(F32) * RAD).astype(jnp.int32)
    rad = (rad[0:2] << 16) | rad[2:4]
    for tile in range(rad.shape[1] // TILE):
        row = half_rows + 2 * tile
        send_ref[row : row + 2, :] = rad[:, tile * TILE : (tile + 1) * TILE]


def rows_kernel(list_ref, count_ref, centre_ref, geo_ref, facing_ref, place_ref, columns):
    group = lax.axis_index("cols")
    columns[...] = jnp.zeros_like(columns)
    lane_row = lax.broadcasted_iota(jnp.int32, (8, TILE), 0)
    ones = jnp.where(lane_row < 3, 1.0, 0.0).astype(F32)
    blank = jnp.zeros((8, TILE), F32)

    def one_slot(slot, carry):
        start = pl.multiple_of(list_ref[group, 0, slot] * TILE, TILE)
        slab = [geo_ref[field, :, pl.ds(start, TILE)] for field in range(5)]
        place = [slab[axis] - centre_ref[axis : axis + 1, :] for axis in range(3)]
        sine = jnp.sin(slab[3])
        normal = (sine * jnp.cos(slab[4]), sine * jnp.sin(slab[4]), jnp.cos(slab[3]))
        shift = -(normal[0] * place[0] + normal[1] * place[1] + normal[2] * place[2])
        square = place[0] * place[0] + place[1] * place[1] + place[2] * place[2]

        def put(row, value):
            columns[pl.ds(row, POINTS, stride=64), :] = value.astype(F32)

        for axis in range(3):
            for part, value in enumerate(parts3(normal[axis])):
                put(8 * part + axis, value)
            for part, value in enumerate(parts3(place[axis])):
                put(32 + 8 * part + axis, value)
        for part, value in enumerate(parts3(shift)):
            put(24 + part, value)
        for part, value in enumerate(parts3(square)):
            put(56 + part, value)
        for point in range(POINTS):
            block = [columns[64 * point + 8 * i : 64 * point + 8 * i + 8, :] for i in range(8)]
            n1, n2, n3, c, x1, x2, x3, q = block
            facing = jnp.concatenate([n1, n1, n1, n2, n2, n3, c, blank], axis=0)
            places = jnp.concatenate([q, x1, x1, x1, x2, x2, x3, ones], axis=0)
            at = pl.ds(point * TILE, TILE)
            facing_ref[slot, at, :] = facing.T.astype(BF16)
            place_ref[slot, at, :] = places.T.astype(BF16)
        return carry

    lax.fori_loop(0, count_ref[group], one_slot, 0)


def main_kernel(
    half_tiles,
    out_tiles,
    list_ref,
    count_ref,
    static_ref,
    spot_ref,
    array_spot_ref,
    centre_ref,
    facing_ref,
    place_ref,
    visible_ref,
    rad_ref,
    own_ref,
    other_ref,
    tiles_ref,
    keep_ref,
    send_ref,
    words,
    total,
):
    group = lax.axis_index("cols")
    lower = lax.axis_index("rows") & 1
    half_rows = 12 * half_tiles + REFS
    total[...] = jnp.zeros_like(total)

    def radiosity(spot):
        pair = rad_ref[pl.ds(2 * spot, 2), :]
        both = jnp.concatenate([pair >> 16, pair & 65535], axis=0)
        return (both.astype(F32) * (1.0 / RAD)).astype(BF16)

    def one_tile(index, carry):
        part = lax.dot_general(
            radiosity(spot_ref[index]), tiles_ref[index], NT, preferred_element_type=F32
        )
        row = static_ref[0, index]
        total[row] = total[row] + part
        return carry

    lax.fori_loop(0, tiles_ref.shape[0], one_tile, 0, unroll=4)

    words[0, 0:half_rows, :] = own_ref[...]
    words[1, 0:half_rows, :] = other_ref[...]
    sub = lax.broadcasted_iota(jnp.int32, (8, POINTS * TILE), 0)
    valid = sub < 3
    away = own_ref[half_rows - REFS :, :].astype(F32) - centre_ref[...]
    away = jnp.concatenate([away] * POINTS, axis=1)
    blank = jnp.zeros((8, POINTS * TILE), F32)
    ones = jnp.where(valid, 1.0, 0.0).astype(F32)

    def stack3(value):
        first, second, third = parts3(value)
        first, second, third = first.astype(F32), second.astype(F32), third.astype(F32)
        return jnp.where(sub == 0, first, jnp.where(sub == 1, second, jnp.where(valid, third, 0.0)))

    def split(value):
        return [part.astype(F32) for part in parts3(value)]

    def one_slot(slot, carry):
        tile = list_ref[group, 1, slot]
        half = (tile // half_tiles) ^ lower
        start = (tile % half_tiles) * 12
        word = jnp.concatenate(
            [words[half, pl.ds(start + point, 8, stride=POINTS), :] for point in range(POINTS)],
            axis=1,
        )
        place = jnp.where(valid, (word >> 16).astype(F32) * (1.0 / POS) + away, 0.0)
        moment = jnp.where(valid, ((word << 16) >> 16).astype(F32) * (1.0 / MOM), 0.0)
        area = jnp.sqrt(jnp.sum(moment * moment, axis=0, keepdims=True))
        shift = stack3(-jnp.sum(moment * place, axis=0, keepdims=True))
        square = stack3(jnp.sum(place * place, axis=0, keepdims=True) + area)
        x1, x2, x3 = split(place)
        m1, m2, m3 = split(moment)
        y1, y2, y3 = -2.0 * x1, -2.0 * x2, -2.0 * x3
        right_f = jnp.concatenate([x1, x2, x3, x1, x2, x1, ones, blank], axis=0).astype(BF16)
        right_t = jnp.concatenate([blank, m1, m2, m3, m1, m2, m1, shift], axis=0).astype(BF16)
        right_s = jnp.concatenate([ones, y1, y2, y3, y1, y2, y1, square], axis=0).astype(BF16)
        gain = None
        for point in range(POINTS):
            left_f = facing_ref[slot, point * TILE : (point + 1) * TILE, :]
            left_x = place_ref[slot, point * TILE : (point + 1) * TILE, :]
            facing = jnp.dot(left_f, right_f, preferred_element_type=F32)
            toward = jnp.dot(left_x, right_t, preferred_element_type=F32)
            spread = jnp.dot(left_x, right_s, preferred_element_type=F32)
            over = jnp.maximum(facing, 0.0) * jnp.maximum(toward, 0.0)
            under = spread * spread
            for first, second in ((0, 1), (2, 3)):
                a = slice(first * TILE, (first + 1) * TILE)
                b = slice(second * TILE, (second + 1) * TILE)
                term = (over[:, a] * under[:, b] + over[:, b] * under[:, a]) / (
                    under[:, a] * under[:, b]
                )
                gain = term if gain is None else gain + term
        gain = gain * visible_ref[slot].astype(F32)
        high = gain.astype(BF16)
        low = (gain - high.astype(F32)).astype(BF16)
        rad = radiosity(array_spot_ref[slot])
        part = lax.dot_general(rad, high, NT, preferred_element_type=F32)
        part = part + lax.dot_general(rad, low, NT, preferred_element_type=F32)
        row = list_ref[group, 0, slot]
        total[row] = total[row] + part * (1.0 / (math.pi * POINTS))
        return carry

    lax.fori_loop(0, count_ref[group], one_slot, 0)
    for tile in range(out_tiles):
        at = slice(tile * TILE, (tile + 1) * TILE)
        keep_ref[:, at] = total[group * out_tiles + tile]
        send_ref[:, at] = total[(1 - group) * out_tiles + tile]


def body(
    radiosity,
    emission,
    material,
    reflectance,
    static_tiles,
    static_index,
    row_geometry,
    array_geometry,
    array_owner,
    array_index,
    array_count,
    visibility,
):
    rows = lax.axis_size("rows")
    me = lax.axis_index("rows")
    owner = array_owner[0]
    bands, patches = radiosity.shape
    own_tiles = patches // TILE
    row_tiles = row_geometry.shape[2] // TILE
    array_tiles = array_geometry.shape[-1] // TILE
    half_tiles = array_tiles // 2
    half_rows = 12 * half_tiles + REFS
    rad_rows = 2 * own_tiles
    slots = visibility.shape[2]
    column_tiles = own_tiles * rows

    spread_bits = [rows >> shift for shift in range(1, rows.bit_length() - 1)]
    order = [1] + spread_bits

    def hop(value, bit):
        return lax.ppermute(value, "rows", [(i, i ^ bit) for i in range(rows)])

    def better(mine, theirs, bit):
        return jnp.where(((owner ^ me) & bit) != 0, theirs, mine)

    keep, send = pl.pallas_call(
        functools.partial(encode_kernel, half_tiles),
        out_shape=(
            jax.ShapeDtypeStruct((half_rows, TILE), jnp.int32),
            jax.ShapeDtypeStruct((half_rows + rad_rows, TILE), jnp.int32),
        ),
        in_specs=[whole(), whole()],
        out_specs=(whole(), whole()),
        scratch_shapes=[VMEM((2, half_rows, TILE), jnp.int32)],
        name="encode",
    )(array_geometry[0, 0], radiosity)

    rad = send[half_rows:]
    for bit in order:
        got = hop(send, bit)
        keep = better(keep, got[:half_rows], bit)
        rad = jnp.concatenate([rad, got[half_rows:]], axis=0)
        send = jnp.concatenate([keep, rad], axis=0)
    other = hop(keep, 1)

    def spot(column_tile):
        holder = (column_tile // own_tiles) ^ me
        place = jnp.zeros_like(column_tile)
        for level, bit in enumerate(order):
            place = place + jnp.where((holder & bit) != 0, 1 << level, 0)
        return place * own_tiles + column_tile % own_tiles

    group = lax.axis_index("cols")
    lists = array_index[0]
    counts = array_count[0]
    static_list = static_index[0, 0]
    static_spot = spot(static_list[1])
    array_spot = spot(column_tiles - array_tiles + lists[group, 1])
    row_centre = jnp.round(row_geometry[0:3, 0, 0])
    row_centre = jnp.pad(jnp.broadcast_to(row_centre[:, None], (3, TILE)), ((0, 5), (0, 0)))

    facing, place = pl.pallas_call(
        rows_kernel,
        out_shape=(jax.ShapeDtypeStruct((slots, POINTS * TILE, 64), BF16),) * 2,
        in_specs=[whole(pltpu.SMEM), whole(pltpu.SMEM), whole(), whole()],
        out_specs=(whole(), whole()),
        scratch_shapes=[VMEM((POINTS * 64, TILE), F32)],
        name="rows",
    )(lists, counts, row_centre, row_geometry)

    onehot = (jnp.arange(reflectance.shape[1], dtype=jnp.int32)[:, None] == material[None, :]).astype(F32)
    albedo = jnp.dot(reflectance, onehot, precision=lax.Precision.HIGHEST)

    shape = jax.ShapeDtypeStruct((bands, patches), F32)
    smem = whole(pltpu.SMEM)
    kept, sent = pl.pallas_call(
        functools.partial(main_kernel, half_tiles, row_tiles // 2),
        out_shape=(shape, shape),
        in_specs=[smem] * 5 + [whole()] * 8,
        out_specs=(whole(), whole()),
        scratch_shapes=[
            VMEM((2, half_rows + 16, TILE), jnp.int32),
            VMEM((row_tiles, bands, TILE), F32),
        ],
        compiler_params=pltpu.CompilerParams(vmem_limit_bytes=40 << 20),
        name="main",
    )(
        lists,
        counts,
        static_list,
        static_spot,
        array_spot,
        row_centre,
        facing,
        place,
        visibility[0, 0],
        rad,
        keep,
        other,
        static_tiles[0, 0],
    )
    arrived = lax.ppermute(sent, "cols", [(0, 1), (1, 0)])
    return emission + albedo * (kept + arrived)


def solution(mesh):
    in_specs = (
        P(None, ("groups", "rows", "cols")),
        P(None, ("groups", "rows", "cols")),
        P(("groups", "rows", "cols")),
        P(),
        P(("groups", "rows"), "cols", None, None, None),
        P(("groups", "rows"), "cols", None, None),
        P(None, None, ("groups", "rows")),
        P(("groups", "cols"), "rows", None, None, None),
        P(("groups", "cols")),
        P(("groups", "rows"), None, None, None),
        P(("groups", "rows"), None),
        P(("groups", "rows"), "cols", None, None, None),
    )
    out_specs = P(None, ("groups", "rows", "cols"))
    return jax.shard_map(body, mesh=mesh, in_specs=in_specs, out_specs=out_specs, check_vma=False)
```

time: 205 us -> 51.9 us (0.25)
  the two profiles are of different devices: /device:TPU:0 before, /device:TPU:27 now
where the time goes in v1:
time: 51.9 us; the launch traced here: 51 us
  waiting for transfers between devices  16.1 us (31%)
  starting transfers between devices  13.4 us (26%)
  Pallas kernels  12.1 us (23%)
  local copies, waits for them, and re-layouts  4.67 us (9%)
  other arithmetic  3.82 us (7%)
  between operations  0.79 us (2%)
    ppermute x4, waiting for transfers between devices, hop(): return lax.ppermute(value, 'rows', [(i, i ^ bit) for i in range(rows)])  15.5 us
    ppermute x1, starting transfers between devices, body(): arrived = lax.ppermute(sent, 'cols', [(0, 1), (1, 0)])  11.9 us
    pallas_call x1, Pallas kernels, body(): pl.pallas_call(functools.partial(main_kernel, half_tiles, row_tiles // 2)...  5.75 us
    pallas_call x1, Pallas kernels, body(): pl.pallas_call(rows_kernel, out_shape=(jax.ShapeDtypeStruct((slots, POINT...  3.71 us
    unnamed x22, local copies, waits for them, and re-layouts  3.21 us
    pallas_call x1, Pallas kernels, body(): pl.pallas_call(functools.partial(encode_kernel, half_tiles), out_shape=(j...  2.59 us
    ppermute x4, starting transfers between devices, hop(): return lax.ppermute(value, 'rows', [(i, i ^ bit) for i in range(rows)])  1.44 us
  transfers between devices with their start and end apart: 5, of which 5 were waited for; matrix products, arithmetic and copies ran while one was open for 6% of the time, Pallas kernels for 7%

profile of v1, /device:TPU:27, one launch (start us, length us, event | category | flops | bytes accessed | tf_op | source)
XLA Modules:
  0.0 51.0 jit_solution(4342627500378193953)
XLA Ops:
  0.0 2.6 %encode.1 = (s32[200,128]{1,0:T(8,128)}, s32[248,128]{1,0:T(8,128)}) custom-call(f32[6,4,4096]{2,1,0:T(4,128)} %bitcast.48, bf16[4,3072]{1,0:T(4,128)(2,1)} %rad_ref.1), custom_call_target="tpu_custom_call" | custom-call | tf_op jit(solution)/shard_map/encode/pallas_call | solution.py:262
  2.6 1.2 %collective-permute-start = (s32[248,128]{1,0:T(8,128)}, s32[248,128]{1,0:T(8,128)S(1)}, u32[]{:S(2)}, u32[]{:S(2)}) collective-permute-start(s32[248,128]{1,0:T(8,128)} %get-tuple-element.13), channel_id=1, source_target_pairs={{0,2},{2,0},{4,6},{6,4},{8,10},{10,8},{12,14},{14,12},{1,3},{3,1},... | collective-permute-start | bytes 380936 | tf_op jit(solution)/shard_map/ppermute | solution.py:257
  3.9 0.8 %slice.30 = s32[48,128]{1,0:T(8,128)S(1)} slice(s32[248,128]{1,0:T(8,128)} %get-tuple-element.13), slice={[200:248], [0:128]} | slice | bytes 49152 | tf_op jit(solution)/shard_map/slice | solution.py:274
  5.3 1.8 %collective-permute-done = s32[248,128]{1,0:T(8,128)S(1)} collective-permute-done((s32[248,128]{1,0:T(8,128)}, s32[248,128]{1,0:T(8,128)S(1)}, u32[]{:S(2)}, u32[]{:S(2)}) %collective-permute-start) | collective-permute-done | bytes 127008 | tf_op jit(solution)/shard_map/ppermute | solution.py:257
  7.1 0.9 %slice_select_fusion.2 = s32[200,128]{1,0:T(8,128)S(1)} fusion(s32[200,128]{1,0:T(8,128)} %get-tuple-element.14, s32[248,128]{1,0:T(8,128)S(1)} %collective-permute-done, pred[]{:T(512)S(6)} %ne.94), kind=kLoop, calls=%fused_computation.7 | loop fusion | flops 25600 | bytes 307201 | tf_op jit(solution)/shard_map/jit(_where)/select_n | solution.py:260
  8.0 0.7 %pad_add_fusion.2 = s32[296,128]{1,0:T(8,128)} fusion(s32[48,128]{1,0:T(8,128)S(1)} %slice.37, s32[48,128]{1,0:T(8,128)S(1)} %slice.30, s32[200,128]{1,0:T(8,128)S(1)} %slice_select_fusion.2), kind=kLoop, calls=%fused_computation.4 | loop fusion | flops 75776 | bytes 303104 | tf_op jit(solution)/shard_map/concatenate | solution.py:279
  8.7 0.1 collective-permute-start.1
  8.8 0.8 %round-nearest-even_reduce_fusion = f32[3]{0:T(128)S(1)} fusion(f32[6,4,6144]{2,1,0:T(4,128)} %geo_ref.1), kind=kLoop, calls=%fused_computation.22 | loop fusion | flops 3 | bytes 24 | tf_op jit(solution)/shard_map/jit(round)/round | solution.py:295
  9.6 0.7 %pad.7.centre_ref = f32[8,128]{1,0:T(8,128)} broadcast(f32[8]{0:T(128)S(1)} %pad.6), dimensions={0} | broadcast | bytes 4128 | tf_op jit(solution)/shard_map/jit(_pad)/pad | solution.py:296
  10.2 3.7 %rows.1 = (bf16[16,512,64]{2,1,0:T(8,128)(2,1)}, bf16[16,512,64]{2,1,0:T(8,128)(2,1)}) custom-call(s32[2,2,16]{2,1,0:T(2,128)} %bitcast.43, s32[2]{0:T(128)} %bitcast.45, f32[8,128]{1,0:T(8,128)} %pad.7.centre_ref, f32[6,4,6144]{2,1,0:T(4,128)} %geo_ref.1), custom_call_target="tpu_custom_call" | custom-call | tf_op jit(solution)/shard_map/rows/pallas_call | solution.py:298
  14.0 0.7 %fusion.4.array_spot_ref = s32[16]{0:T(128)S(1)} fusion(s32[1,2,2,16]{3,2,1,0:T(2,128)} %param.21, s32[]{:T(128)S(6)} %select_n.71, s32[]{:T(128)S(6)} %axis_index.23), kind=kLoop, calls=%fused_computation.24 | loop fusion | flops 432 | bytes 136 | tf_op jit(solution)/shard_map/add | solution.py:287
  14.7 4.2 %collective-permute-done.1 = s32[296,128]{1,0:T(8,128)S(1)} collective-permute-done((s32[296,128]{1,0:T(8,128)}, s32[296,128]{1,0:T(8,128)S(1)}, u32[]{:S(2)}, u32[]{:S(2)}) %collective-permute-start.1) | collective-permute-done | bytes 151584 | tf_op jit(solution)/shard_map/ppermute | solution.py:257
  18.9 0.1 collective-permute-start.2
  19.0 6.0 %collective-permute-done.2 = s32[392,128]{1,0:T(8,128)S(1)} collective-permute-done((s32[392,128]{1,0:T(8,128)S(1)}, s32[392,128]{1,0:T(8,128)S(1)}, u32[]{:S(2)}, u32[]{:S(2)}) %collective-permute-start.2) | collective-permute-done | bytes 200736 | tf_op jit(solution)/shard_map/ppermute | solution.py:257
  25.0 0.1 collective-permute-start.3
  25.1 3.5 %collective-permute-done.3.other_ref = s32[200,128]{1,0:T(8,128)S(1)} collective-permute-done((s32[200,128]{1,0:T(8,128)S(1)}, s32[200,128]{1,0:T(8,128)S(1)}, u32[]{:S(2)}, u32[]{:S(2)}) %collective-permute-start.3) | collective-permute-done | bytes 102432 | tf_op jit(solution)/shard_map/ppermute | solution.py:257
  28.6 0.0 copy-done.4
  28.6 1.6 %copy-done.2 = bf16[16,512,64]{2,1,0:T(8,128)(2,1)S(1)} copy-done((bf16[16,512,64]{2,1,0:T(8,128)(2,1)S(1)}, bf16[16,512,64]{2,1,0:T(8,128)(2,1)}, u32[]{:S(2)}) %copy-start.2) | copy-done | bytes 1048600
  30.2 1.6 %copy-done.3 = bf16[16,512,64]{2,1,0:T(8,128)(2,1)S(1)} copy-done((bf16[16,512,64]{2,1,0:T(8,128)(2,1)S(1)}, bf16[16,512,64]{2,1,0:T(8,128)(2,1)}, u32[]{:S(2)}) %copy-start.3) | copy-done | bytes 1048600
  31.8 5.8 %main.1 = (f32[4,3072]{1,0:T(4,128)S(1)}, f32[4,3072]{1,0:T(4,128)S(1)}) custom-call(s32[2,2,16]{2,1,0:T(2,128)S(1)} %bitcast.44, s32[2]{0:T(128)S(1)} %bitcast.46, s32[2,64]{1,0:T(2,128)S(1)} %bitcast.47, s32[64]{0:T(128)S(1)} %fusion.3.spot_ref, s32[16]{0:T(128)S(1)} %fusion.4.array_spot_ref, f32[8,128]{1,0:T(8,128)S(1)} %copy-done.5, ...), custom_call_target="tpu_custom_call" | custom-call | tf_op jit(solution)/shard_map/main/pallas_call | solution.py:312
  37.6 11.9 %collective-permute-start.4 = (f32[4,3072]{1,0:T(4,128)S(1)}, f32[4,3072]{1,0:T(4,128)S(1)}, u32[]{:S(2)}, u32[]{:S(2)}) collective-permute-start(f32[4,3072]{1,0:T(4,128)S(1)} %get-tuple-element.16), channel_id=1, source_target_pairs={{0,1},{1,0},{2,3},{3,2},{4,5},{5,4},{6,7},{7,6},{8,9},{9,8},{10,11... | collective-permute-start | bytes 147464 | tf_op jit(solution)/shard_map/ppermute | solution.py:338
  49.5 0.2 convolution_bitcast_fusion
  49.7 0.7 %collective-permute-done.4 = f32[4,3072]{1,0:T(4,128)S(1)} collective-permute-done((f32[4,3072]{1,0:T(4,128)S(1)}, f32[4,3072]{1,0:T(4,128)S(1)}, u32[]{:S(2)}, u32[]{:S(2)}) %collective-permute-start.4) | collective-permute-done | bytes 49184 | tf_op jit(solution)/shard_map/ppermute | solution.py:338
  50.4 0.6 %multiply_add_fusion = f32[4,3072]{1,0:T(4,128)} fusion(f32[4,3072]{1,0:T(4,128)S(1)} %copy-done.9, f32[4,3072]{1,0:T(4,128)S(1)} %convolution_bitcast_fusion, f32[4,3072]{1,0:T(4,128)S(1)} %get-tuple-element.15, f32[4,3072]{1,0:T(4,128)S(1)} %collective-permute-done.4), kind=kLoop, calls=%fused_computation.9 | loop fusion | flops 36864 | bytes 245760 | tf_op jit(solution)/shard_map/add | solution.py:339
  (28 shorter events, 0.1 us)
Async XLA Ops:
  0.0 49.5 %copy-start = (f32[4,16]{1,0:T(4,128)S(1)}, f32[4,16]{1,0:T(4,128)}, u32[]{:S(2)}) copy-start(f32[4,16]{1,0:T(4,128)} %param.15) | copy-start | bytes 772
  0.0 28.6 %copy-start.6 = (s32[1,2,2,16]{3,2,1,0:T(2,128)S(1)}, s32[1,2,2,16]{3,2,1,0:T(2,128)}, u32[]{:S(2)}) copy-start(s32[1,2,2,16]{3,2,1,0:T(2,128)} %param.21) | copy-start | bytes 772
  0.0 28.6 %copy-start.7 = (s32[1,2]{1,0:T(1,128)S(1)}, s32[1,2]{1,0:T(1,128)}, u32[]{:S(2)}) copy-start(s32[1,2]{1,0:T(1,128)} %param.22) | copy-start | bytes 28
  0.0 18.9 %copy-start.8 = (s32[1,1,2,64]{3,2,1,0:T(2,128)S(1)}, s32[1,1,2,64]{3,2,1,0:T(2,128)}, u32[]{:S(2)}) copy-start(s32[1,1,2,64]{3,2,1,0:T(2,128)} %param.17) | copy-start | bytes 1540
  0.0 28.6 %copy-start.4 = (s32[1,1,16,128,128]{4,3,2,1,0:T(8,128)S(1)}, s32[1,1,16,128,128]{4,3,2,1,0:T(8,128)}, u32[]{:S(2)}) copy-start(s32[1,1,16,128,128]{4,3,2,1,0:T(8,128)} %param.23) | copy-start | bytes 3145732
  0.0 28.6 %copy-start.1 = (bf16[1,1,64,128,128]{4,3,2,1,0:T(8,128)(2,1)S(1)}, bf16[1,1,64,128,128]{4,3,2,1,0:T(8,128)(2,1)}, u32[]{:S(2)}) copy-start(bf16[1,1,64,128,128]{4,3,2,1,0:T(8,128)(2,1)} %param.16) | copy-start | bytes 6291460
  2.6 4.5 %collective-permute-start = (s32[248,128]{1,0:T(8,128)}, s32[248,128]{1,0:T(8,128)S(1)}, u32[]{:S(2)}, u32[]{:S(2)}) collective-permute-start(s32[248,128]{1,0:T(8,128)} %get-tuple-element.13), channel_id=1, source_target_pairs={{0,2},{2,0},{4,6},{6,4},{8,10},{10,8},{12,14},{14,12},{1,3},{3,1},... | collective-permute-start | bytes 380936 | tf_op jit(solution)/shard_map/ppermute | solution.py:257
  8.7 10.1 %collective-permute-start.1 = (s32[296,128]{1,0:T(8,128)}, s32[296,128]{1,0:T(8,128)S(1)}, u32[]{:S(2)}, u32[]{:S(2)}) collective-permute-start(s32[296,128]{1,0:T(8,128)} %pad_add_fusion.2), channel_id=1, source_target_pairs={{0,8},{2,10},{4,12},{6,14},{8,0},{10,2},{12,4},{14,6},{1,9},{3,11}... | collective-permute-start | bytes 454664 | tf_op jit(solution)/shard_map/ppermute | solution.py:257
  10.2 18.4 %copy-start.5 = (f32[8,128]{1,0:T(8,128)S(1)}, f32[8,128]{1,0:T(8,128)}, u32[]{:S(2)}) copy-start(f32[8,128]{1,0:T(8,128)} %pad.7.centre_ref) | copy-start | bytes 12292
  18.9 6.1 %collective-permute-start.2 = (s32[392,128]{1,0:T(8,128)S(1)}, s32[392,128]{1,0:T(8,128)S(1)}, u32[]{:S(2)}, u32[]{:S(2)}) collective-permute-start(s32[392,128]{1,0:T(8,128)S(1)} %pad_add_fusion), channel_id=1, source_target_pairs={{0,4},{2,6},{4,0},{6,2},{8,12},{10,14},{12,8},{14,10},{1,5},{3,7},... | collective-permute-start | bytes 602120 | tf_op jit(solution)/shard_map/ppermute | solution.py:257
  25.0 3.6 %collective-permute-start.3 = (s32[200,128]{1,0:T(8,128)S(1)}, s32[200,128]{1,0:T(8,128)S(1)}, u32[]{:S(2)}, u32[]{:S(2)}) collective-permute-start(s32[200,128]{1,0:T(8,128)S(1)} %slice_select_fusion.own_ref), channel_id=1, source_target_pairs={{0,2},{2,0},{4,6},{6,4},{8,10},{10,8},{12,14},{14,12},{1,3},{3,1},... | collective-permute-start | bytes 307208 | tf_op jit(solution)/shard_map/ppermute | solution.py:257
  28.6 1.6 %copy-start.2 = (bf16[16,512,64]{2,1,0:T(8,128)(2,1)S(1)}, bf16[16,512,64]{2,1,0:T(8,128)(2,1)}, u32[]{:S(2)}) copy-start(bf16[16,512,64]{2,1,0:T(8,128)(2,1)} %get-tuple-element.11.facing_ref) | copy-start | bytes 3145732
  30.2 1.6 %copy-start.3 = (bf16[16,512,64]{2,1,0:T(8,128)(2,1)S(1)}, bf16[16,512,64]{2,1,0:T(8,128)(2,1)}, u32[]{:S(2)}) copy-start(bf16[16,512,64]{2,1,0:T(8,128)(2,1)} %get-tuple-element.12.place_ref) | copy-start | bytes 3145732
  31.8 17.7 %copy-start.10 = (s32[3072]{0:T(1024)S(1)}, s32[3072]{0:T(1024)}, u32[]{:S(2)}) copy-start(s32[3072]{0:T(1024)} %param.14) | copy-start | bytes 36868
  31.8 18.6 %copy-start.9 = (f32[4,3072]{1,0:T(4,128)S(1)}, f32[4,3072]{1,0:T(4,128)}, u32[]{:S(2)}) copy-start(f32[4,3072]{1,0:T(4,128)} %param.13) | copy-start | bytes 147460
  37.6 12.8 %collective-permute-start.4 = (f32[4,3072]{1,0:T(4,128)S(1)}, f32[4,3072]{1,0:T(4,128)S(1)}, u32[]{:S(2)}, u32[]{:S(2)}) collective-permute-start(f32[4,3072]{1,0:T(4,128)S(1)} %get-tuple-element.16), channel_id=1, source_target_pairs={{0,1},{1,0},{2,3},{3,2},{4,5},{5,4},{6,7},{7,6},{8,9},{9,8},{10,11... | collective-permute-start | bytes 147464 | tf_op jit(solution)/shard_map/ppermute | solution.py:338
